TPU v7x, 512 devices: a whole 4x4x16 slice. The times are simulated.
512 devices in a mesh: group: 8 (over z_lo), shard: 64 (over z_hi, x, y, core).
Axes of the slice: x: 4, y: 4, z: 16 (z_hi: 2, z_lo: 8; z = z_hi * 8 + z_lo), core: 2. Of those that a mesh axis runs over, the one named last changes fastest.
Arguments:
- inner_embed: float32 [8, 15360, 768], P('group', 'shard'), may hold values from -6 to 6
- outer_embed: float32 [15360, 768], P('shard'), may hold values from -6 to 6
- moment_embed: float32 [15360, 768], P('shard'), may hold values from -6 to 6
- basis: float32 [15360, 64], P('shard'), may hold values from -6 to 6
- inner_attn: float32 [8, 768, 3072], P('group', 'shard'), may hold values from -6 to 6
- outer_attn: float32 [768, 3072], P(None, 'shard'), may hold values from -6 to 6
- moment_attn: float32 [768, 3072], P(None, 'shard'), may hold values from -6 to 6
- inner_norms: float32 [8, 4, 768], P('group', None, 'shard'), may hold values from -6 to 6
- outer_norms: float32 [4, 768], P(None, 'shard'), may hold values from -6 to 6
- moment_norms: float32 [4, 768], P(None, 'shard'), may hold values from -6 to 6
Outputs:
- new_embed: float32 [15360, 768], P('shard')
- new_moment_embed: float32 [15360, 768], P('shard')
- new_attn: float32 [768, 3072], P(None, 'shard')
- new_moment_attn: float32 [768, 3072], P(None, 'shard')
- new_norms: float32 [4, 768], P(None, 'shard')
- new_moment_norms: float32 [4, 768], P(None, 'shard')
- replica_attn: bfloat16 [768, 3072], P('shard')
All inputs are finite; a program needn't handle non-finite values.
Results may differ from a plain program's by a relative error of at most 0.0004.
Values may be sent and summed in bfloat16 or wider, within the bound.
A program may use at most 64 MiB of HBM per device.

v0:
```python
import math

import jax
import jax.numpy as jnp
from jax import lax
from jax.sharding import PartitionSpec as P

VOCAB = 15360
RANK = 64


def nesterov(outer, moment, delta):
    moment_new = 0.5 * moment + delta
    return (outer - (delta + 0.5 * moment_new), moment_new)


def on_device(
    inner_embed,
    outer_embed,
    moment_embed,
    basis,
    inner_attn,
    outer_attn,
    moment_attn,
    inner_norms,
    outer_norms,
    moment_norms,
):
    groups = lax.axis_size("group")
    embed_diff = outer_embed - inner_embed[0]
    partial_coeff = lax.dot_general(
        basis,
        embed_diff,
        (((0,), (0,)), ((), ())),
        precision=lax.Precision.HIGHEST,
        preferred_element_type=jnp.float32,
    )
    norm_diff = outer_norms - inner_norms[0]
    moved = lax.all_to_all(inner_attn[0], "shard", split_axis=1, concat_axis=0, tiled=True)
    attn_term = outer_attn - moved
    coeff_sum = lax.psum(partial_coeff, ("group", "shard"))
    attn_sum, norm_sum = lax.psum((attn_term, norm_diff), "group")
    attn_delta = attn_sum / groups
    norm_delta = norm_sum / groups
    coefficient = coeff_sum / groups
    embed_delta = jnp.dot(
        basis, coefficient, precision=lax.Precision.HIGHEST, preferred_element_type=jnp.float32
    ) * (1.0 / math.sqrt(RANK * VOCAB))
    new_embed, new_moment_embed = nesterov(outer_embed, moment_embed, embed_delta)
    new_attn, new_moment_attn = nesterov(outer_attn, moment_attn, attn_delta)
    new_norms, new_moment_norms = nesterov(outer_norms, moment_norms, norm_delta)
    replica_attn = lax.all_to_all(
        new_attn.astype(jnp.bfloat16), "shard", split_axis=0, concat_axis=1, tiled=True
    )
    return (
        new_embed,
        new_moment_embed,
        new_attn,
        new_moment_attn,
        new_norms,
        new_moment_norms,
        replica_attn,
    )


def solution(mesh):
    placed = (
        P("group", "shard", None),
        P("shard", None),
        P("shard", None),
        P("shard", None),
        P("group", "shard", None),
        P(None, "shard"),
        P(None, "shard"),
        P("group", None, "shard"),
        P(None, "shard"),
        P(None, "shard"),
    )
    return jax.shard_map(
        on_device,
        mesh=mesh,
        in_specs=placed,
        out_specs=(
            P("shard", None),
            P("shard", None),
            P(None, "shard"),
            P(None, "shard"),
            P(None, "shard"),
            P(None, "shard"),
            P("shard", None),
        ),
        check_vma=False,
    )
```

profile of v0, /device:TPU:1, one launch (start us, length us, event | category | flops | bytes accessed | tf_op | source)
XLA Modules:
  0.0 638.4 jit_solution(14730503204910227283)
XLA Ops:
  7.2 0.0 copy-start
  7.2 1.3 reduce
  8.5 0.2 all_to_all.28
  8.7 0.2 copy.34
  8.9 1.0 reshape.22
  9.9 0.0 copy-start.4
  9.9 22.4 %all-to-all-start = ((f32[64,1,576]{2,1,0:T(1,128)}), f32[64,1,576]{2,1,0:T(1,128)S(1)}, u32[]{:S(2)}, u32[]{:S(2)}) async-start(f32[64,1,576]{2,1,0:T(1,128)} %reshape.22), calls=%async_computation | async-start | bytes 327680 | tf_op jit(solution)/shard_map/all_to_all | solution.py:39
  32.3 0.0 all-reduce.5.cloned.1.call-start
  32.4 0.0 copy-done.4
  32.4 0.2 copy.29
  32.6 17.3 %all-to-all-done = f32[64,1,576]{2,1,0:T(1,128)S(1)} async-done(((f32[64,1,576]{2,1,0:T(1,128)}), f32[64,1,576]{2,1,0:T(1,128)S(1)}, u32[]{:S(2)}, u32[]{:S(2)}) %all-to-all-start) | async-done | bytes 147488 | tf_op jit(solution)/shard_map/all_to_all | solution.py:39
  49.9 0.5 broadcast.29
  50.4 1.0 reduce.1
  51.4 0.2 reshape.23
  51.7 0.0 copy-start.1
  51.7 0.0 copy-start.2
  51.7 0.8 sub.20
  52.5 0.0 all-reduce.5.cloned.1.call-update
  52.5 0.0 all-reduce.3.cloned.1.call-start
  52.6 0.0 copy-done
  52.6 0.4 copy-done.1
  53.0 0.2 copy-done.2
  53.2 1.3 convolution_bitcast_fusion
  54.5 0.0 copy-start.5
  54.5 0.0 all-reduce.3.cloned.1.call-update
  54.5 0.9 copy-done.5
  55.4 0.0 copy-start.6
  55.4 0.2 copy.28
  55.5 0.5 copy-done.6
  56.1 0.0 copy-done.7
  56.1 27.7 %psum.23 = f32[4,12]{1,0:T(4,128)S(1)} all-reduce(f32[4,12]{1,0:T(4,128)S(1)} %bitcast_subtract_fusion.2), channel_id=1, replica_groups=mesh['group'=8,'shard'=64] {'group'}, use_global_device_ids=true, to_apply=%region_2.0 | all-reduce | flops 48 | bytes 384 | tf_op jit(solution)/shard_map/psum | solution.py:42
  83.8 0.0 copy-done.8
  83.8 0.6 add_subtract_fusion.2
  84.4 80.6 %all-reduce.5.cloned.1.call-done = f32[768,48]{1,0:T(8,128)} async-done(((f32[768,48]{1,0:T(8,128)}), f32[768,48]{1,0:T(8,128)}) %all-reduce.5.cloned.1.call-update) | async-done | bytes 147472 | tf_op jit(solution)/shard_map/psum | solution.py:42
  165.0 1.1 fusion.4
  166.1 0.0 copy-start.3
  166.1 0.1 all_to_all.32
  166.2 0.9 reshape.24
  167.1 16.1 %all-to-all-start.1 = ((bf16[64,2,288]{2,1,0:T(2,128)(2,1)}), bf16[64,2,288]{2,1,0:T(2,128)(2,1)S(1)}, u32[]{:S(2)}, u32[]{:S(2)}) async-start(bf16[64,2,288]{2,1,0:T(2,128)(2,1)} %reshape.24), calls=%async_computation.1 | async-start | bytes 196608 | tf_op jit(solution)/shard_map/all_to_all | solution.py:52
  183.3 442.5 %all-reduce.3.cloned.1.call-done = f32[64,768]{1,0:T(8,128)} async-done(((f32[64,768]{1,0:T(8,128)}), f32[64,768]{1,0:T(8,128)}) %all-reduce.3.cloned.1.call-update) | async-done | bytes 196624 | tf_op jit(solution)/shard_map/psum | solution.py:41
  625.8 0.0 copy-done.3
  625.8 2.9 add_subtract_fusion
  628.7 0.8 copy.31
  629.5 0.8 copy.32
  630.3 0.0 all-to-all-done.1
  630.3 0.2 reshape.25
  630.6 0.1 copy.30
  630.6 0.9 all_to_all.35
  (5 shorter events, 0.1 us)
Async XLA Ops:
  7.2 45.4 %copy-start = (f32[240,64]{0,1:T(8,128)S(1)}, f32[240,64]{0,1:T(8,128)}, u32[]{:S(2)}) copy-start(f32[240,64]{0,1:T(8,128)} %param.13) | copy-start | bytes 184324
  9.9 22.4 %copy-start.4 = (f32[768,48]{0,1:T(8,128)S(1)}, f32[768,48]{0,1:T(8,128)}, u32[]{:S(2)}) copy-start(f32[768,48]{0,1:T(8,128)} %param.15) | copy-start | bytes 442372
  9.9 39.9 %all-to-all-start = ((f32[64,1,576]{2,1,0:T(1,128)}), f32[64,1,576]{2,1,0:T(1,128)S(1)}, u32[]{:S(2)}, u32[]{:S(2)}) async-start(f32[64,1,576]{2,1,0:T(1,128)} %reshape.22), calls=%async_computation | async-start | bytes 327680 | tf_op jit(solution)/shard_map/all_to_all | solution.py:39
  32.3 132.7 %all-reduce.5.cloned.1.call-start = ((), (), s32[]{:S(2)}) async-start(), calls=%async_computation.3 | async-start | bytes 786432 | tf_op jit(solution)/shard_map/psum | solution.py:42
  51.7 1.3 copy-start.1
  51.7 1.5 copy-start.2
  52.5 573.3 %all-reduce.3.cloned.1.call-start = ((), (), s32[]{:S(2)}) async-start(), calls=%async_computation.2 | async-start | bytes 393216 | tf_op jit(solution)/shard_map/psum | solution.py:41
  54.5 0.9 copy-start.5
  55.4 0.7 copy-start.6
  55.4 0.7 copy-start.7
  56.1 27.7 %copy-start.8 = (f32[4,12]{1,0:T(4,128)S(1)}, f32[4,12]{1,0:T(4,128)}, u32[]{:S(2)}) copy-start(f32[4,12]{1,0:T(4,128)} %param.19) | copy-start | bytes 580
  166.1 459.7 %copy-start.3 = (f32[240,768]{1,0:T(8,128)S(1)}, f32[240,768]{1,0:T(8,128)}, u32[]{:S(2)}) copy-start(f32[240,768]{1,0:T(8,128)} %param.12) | copy-start | bytes 2211844
  167.1 463.2 %all-to-all-start.1 = ((bf16[64,2,288]{2,1,0:T(2,128)(2,1)}), bf16[64,2,288]{2,1,0:T(2,128)(2,1)S(1)}, u32[]{:S(2)}, u32[]{:S(2)}) async-start(bf16[64,2,288]{2,1,0:T(2,128)(2,1)} %reshape.24), calls=%async_computation.1 | async-start | bytes 196608 | tf_op jit(solution)/shard_map/all_to_all | solution.py:52
Sparse Core Ops, SparseCore 0:
  52.7 112.3 all-reduce.4
  171.9 453.8 all-reduce.2
where the time goes:
time: 639 us; the launch traced here: 638 us
  waiting for transfers between devices  540 us (85%)
  starting transfers between devices  38.6 us (6%)
  blocking collectives  27.7 us (4%)
  between operations  14.2 us (2%)
  local copies, waits for them, and re-layouts  8.4 us (1%)
    psum x1, waiting for transfers between devices, on_device(): coeff_sum = lax.psum(partial_coeff, ('group', 'shard'))  442 us
    psum x1, waiting for transfers between devices, on_device(): attn_sum, norm_sum = lax.psum((attn_term, norm_diff), 'group')  80.6 us
    psum x1, blocking collectives, on_device(): attn_sum, norm_sum = lax.psum((attn_term, norm_diff), 'group')  27.7 us
    all_to_all x1, starting transfers between devices, on_device(): lax.all_to_all(inner_attn[0], 'shard', split_axis=1, concat_axis=0, tiled...  22.4 us
    all_to_all x1, waiting for transfers between devices, on_device(): lax.all_to_all(inner_attn[0], 'shard', split_axis=1, concat_axis=0, tiled...  17.3 us
    all_to_all x1, starting transfers between devices, on_device(): lax.all_to_all(new_attn.astype(jnp.bfloat16), 'shard', split_axis=0, conc...  16.1 us
  transfers between devices with their start and end apart: 4, of which 3 were waited for; matrix products, arithmetic and copies ran while one was open for 1% of the time, Pallas kernels for 0%

commit v1 on v0

v1 whole, which is shorter than its diff:
```python
import math

import jax
import jax.numpy as jnp
from jax import lax
from jax.experimental import pallas as pl
from jax.experimental.pallas import tpu as pltpu
from jax.sharding import PartitionSpec as P

VOCAB = 15360
RANK = 64
D = 768
N = 8
ROWS = 12
COLS = 48
WIDE = N * COLS
TALL = N * ROWS
MESH = pl.DeviceIdType.MESH
HIGHEST = lax.Precision.HIGHEST
SCALE = 1.0 / math.sqrt(RANK * VOCAB)

CA, CB, CG, RB, RA, P1, W, NR, SW, AG, RP = range(11)
(L_IE, L_OE, L_BA, L_ME, L_OA, L_MA, L_IA, L_IN, L_ON, L_MN,
 L_EM, L_AT, L_NO, L_RP) = range(14)


def nesterov(outer, moment, delta):
    moment_new = 0.5 * moment + delta
    return (outer - (delta + 0.5 * moment_new), moment_new)


def kernel(
    inner_e, outer_e, mom_e, basis, inner_a, outer_a, mom_a, inner_n, outer_n, mom_n,
    new_e, new_me, new_a, new_ma, new_n, new_mn, rep,
    v_ie, v_oe, v_me, v_ba, v_oa, v_ma, v_on, v_mn,
    r_norm, c_part, r_ca, c_row, r_cb, c_one, r_cg, c_fin, r_rb, c_blk, r_ra,
    r_p1, w_out, r_w, d_out, r_d, d_pack, r_ag, rp_out, r_rp,
    o_e, o_me, o_a, o_ma, o_n, o_mn, o_rep,
    send, recv, once, local,
):
    g = lax.axis_index("group")
    s = lax.axis_index("shard")
    b = s // N
    a = s % N
    over_g = [(lax.rem(g + k, N), s) for k in range(1, N)]
    over_a = [(g, N * b + lax.rem(a + k, N)) for k in range(1, N)]
    over_b = [(g, N * lax.rem(b + k, N) + a) for k in range(1, N)]
    swapped = [(b, N * g + lax.rem(a + k, N)) for k in range(N)]
    crossing = g != b

    def load(src, dst, sem):
        copy = pltpu.make_async_copy(src, dst, local.at[sem])
        copy.start()
        return copy

    ld_oa = load(outer_a, v_oa, L_OA)
    ld_ma = load(mom_a, v_ma, L_MA)
    ld_ie = load(inner_e.at[0], v_ie, L_IE)
    ld_oe = load(outer_e, v_oe, L_OE)
    ld_ba = load(basis, v_ba, L_BA)
    ld_ia = load(
        inner_a.at[0, :, pl.ds(pl.multiple_of(g * WIDE, 128), WIDE)], r_p1.at[g], L_IA
    )
    ld_in = load(inner_n.at[0], r_norm.at[g], L_IN)
    ld_on = load(outer_n, v_on, L_ON)
    ld_mn = load(mom_n, v_mn, L_MN)
    ld_me = load(mom_e, v_me, L_ME)

    barrier = pltpu.get_barrier_semaphore()

    def greet(device):
        pl.semaphore_signal(barrier, inc=1, device_id=device, device_id_type=MESH)

    for device in over_a + over_g + over_b + swapped[1:]:
        greet(device)

    @pl.when(crossing)
    def _():
        greet(swapped[0])

    def put(src, dst, phase, device, send_sem=None):
        pltpu.make_async_remote_copy(
            src_ref=src,
            dst_ref=dst,
            send_sem=send.at[phase] if send_sem is None else send_sem,
            recv_sem=recv.at[phase],
            device_id=device,
            device_id_type=MESH,
        ).start()

    def whole(ref, phase, count):
        part = ref.at[pl.ds(0, count)]
        return pltpu.make_async_remote_copy(
            src_ref=part,
            dst_ref=part,
            send_sem=send.at[phase],
            recv_sem=recv.at[phase],
            device_id=over_g[0],
            device_id_type=MESH,
        )

    def arrived(ref, phase):
        whole(ref, phase, N - 1).wait_recv()

    def swap(src, dst, phase, turn):
        @pl.when(crossing)
        def _():
            put(src.at[a], dst.at[a], phase, swapped[0], once.at[turn])

        @pl.when(jnp.logical_not(crossing))
        def _():
            dst[a] = src[a]

        for k in range(1, N):
            put(src.at[lax.rem(a + k, N)], dst.at[a], phase, swapped[k])

    def swap_arrived(ref, phase):
        @pl.when(crossing)
        def _():
            whole(ref, phase, N).wait_recv()

        @pl.when(jnp.logical_not(crossing))
        def _():
            arrived(ref, phase)

    ld_oa.wait()
    ld_ma.wait()
    mine = pl.ds(pl.multiple_of(g * TALL, 8), TALL)
    outer_block = v_oa[mine, :]
    mom_block = v_ma[mine, :]
    for j in range(N):
        w_out[j, 0] = outer_block[j * ROWS : (j + 1) * ROWS, :]
        w_out[j, 1] = mom_block[j * ROWS : (j + 1) * ROWS, :]

    ld_ie.wait()
    ld_oe.wait()
    ld_ba.wait()
    v_ie[...] = v_oe[...] - v_ie[...]
    part = lax.dot_general(
        v_ba[...],
        v_ie[...],
        (((0,), (0,)), ((), ())),
        precision=HIGHEST,
        preferred_element_type=jnp.float32,
    )
    c_part[...] = part.reshape(N, N, D)

    pl.semaphore_wait(barrier, 4 * (N - 1) + jnp.where(crossing, 1, 0))

    for k in range(1, N):
        put(c_part.at[lax.rem(a + k, N)], r_ca.at[a], CA, over_a[k - 1])
    for k in range(1, N):
        to = lax.rem(g + k, N)
        put(
            inner_a.at[0, :, pl.ds(pl.multiple_of(to * WIDE, 128), WIDE)],
            r_p1.at[g],
            P1,
            over_g[k - 1],
        )
    swap(w_out, r_w, W, 0)
    for k in range(1, N):
        put(inner_n.at[0], r_norm.at[g], NR, over_g[k - 1])

    r_ca[a] = c_part[a]
    arrived(r_ca, CA)
    rows = r_ca[0]
    for j in range(1, N):
        rows = rows + r_ca[j]
    for j in range(N):
        c_row[j] = rows[j : j + 1, :]
    for k in range(1, N):
        put(c_row.at[lax.rem(b + k, N)], r_cb.at[b], CB, over_b[k - 1])
    r_cb[b] = c_row[b]
    arrived(r_cb, CB)
    row = r_cb[0]
    for j in range(1, N):
        row = row + r_cb[j]
    c_one[0] = row
    r_cg[g] = row
    for k in range(1, N):
        put(c_one.at[0], r_cg.at[g], CG, over_g[k - 1])

    ld_ia.wait()
    arrived(r_p1, P1)
    swap_arrived(r_w, W)
    outer_wide = jnp.concatenate([r_w[j, 0] for j in range(N)], axis=1)
    mom_wide = jnp.concatenate([r_w[j, 1] for j in range(N)], axis=1)
    total = outer_wide - r_p1[0]
    for j in range(1, N):
        total = total + (outer_wide - r_p1[j])
    delta = total * (1.0 / N)
    for j in range(N):
        d_out[j] = delta[:, j * COLS : (j + 1) * COLS]
    swap(d_out, r_d, SW, 1)
    rp_out[0] = nesterov(outer_wide, mom_wide, delta)[0].astype(jnp.bfloat16)
    for k in range(1, N):
        put(rp_out.at[0], r_rp.at[g], RP, over_g[k - 1])
    r_rp[g] = rp_out[0]

    arrived(r_cg, CG)
    row = r_cg[0]
    for j in range(1, N):
        row = row + r_cg[j]
    row = row * (1.0 / N)
    c_fin[0] = row
    r_rb[b] = row
    for k in range(1, N):
        put(c_fin.at[0], r_rb.at[b], RB, over_b[k - 1])

    swap_arrived(r_d, SW)
    pack = jnp.concatenate([r_d[j] for j in range(N)], axis=1)
    d_pack[0] = pack
    r_ag[g] = pack
    for k in range(1, N):
        put(d_pack.at[0], r_ag.at[g], AG, over_g[k - 1])

    arrived(r_rb, RB)
    block = jnp.concatenate([r_rb[j] for j in range(N)], axis=0)
    c_blk[0] = block
    r_ra[a] = block
    for k in range(1, N):
        put(c_blk.at[0], r_ra.at[a], RA, over_a[k - 1])

    ld_in.wait()
    ld_on.wait()
    ld_mn.wait()
    arrived(r_norm, NR)
    outer_norm = v_on[...]
    total = outer_norm - r_norm[0]
    for j in range(1, N):
        total = total + (outer_norm - r_norm[j])
    o_n[...], o_mn[...] = nesterov(outer_norm, v_mn[...], total * (1.0 / N))
    outs = [load(o_n, new_n, L_NO), load(o_mn, new_mn, L_NO + 2)]

    ld_me.wait()
    arrived(r_ra, RA)
    change = jnp.dot(
        v_ba[...],
        r_ra[...].reshape(RANK, D),
        precision=HIGHEST,
        preferred_element_type=jnp.float32,
    ) * SCALE
    o_e[...], o_me[...] = nesterov(v_oe[...], v_me[...], change)
    outs += [load(o_e, new_e, L_IE), load(o_me, new_me, L_OE)]

    arrived(r_rp, RP)
    for j in range(N):
        o_rep[:, j * WIDE : (j + 1) * WIDE] = r_rp[j]
    outs += [load(o_rep, rep, L_RP)]
    arrived(r_ag, AG)
    for j in range(N):
        wide = r_ag[j]
        tall = jnp.concatenate(
            [wide[:, i * COLS : (i + 1) * COLS] for i in range(N)], axis=0
        )
        where = pl.ds(j * TALL, TALL)
        o_a[where, :], o_ma[where, :] = nesterov(v_oa[where, :], v_ma[where, :], tall)
    outs += [load(o_a, new_a, L_OA), load(o_ma, new_ma, L_MA)]

    for ref, phase in (
        (r_ca, CA), (r_cb, CB), (r_cg, CG), (r_rb, RB), (r_ra, RA), (r_p1, P1),
        (r_w, W), (r_norm, NR), (r_d, SW), (r_ag, AG), (r_rp, RP),
    ):
        whole(ref, phase, N - 1).wait_send()

    @pl.when(crossing)
    def _():
        for ref, turn in ((r_w, 0), (r_d, 1)):
            pltpu.make_async_remote_copy(
                src_ref=ref.at[0],
                dst_ref=ref.at[0],
                send_sem=once.at[turn],
                recv_sem=recv.at[W],
                device_id=over_g[0],
                device_id_type=MESH,
            ).wait_send()

    for copy in outs:
        copy.wait()


def on_device(*args):
    f32 = jnp.float32
    shapes = [
        ((240, D), f32), ((240, D), f32), ((D, COLS), f32), ((D, COLS), f32),
        ((4, ROWS), f32), ((4, ROWS), f32), ((ROWS, 4 * D), jnp.bfloat16),
    ]
    vmem = pltpu.VMEM
    return pl.pallas_call(
        kernel,
        out_shape=[jax.ShapeDtypeStruct(*shape) for shape in shapes],
        in_specs=[pl.BlockSpec(memory_space=pl.ANY)] * 10,
        out_specs=[pl.BlockSpec(memory_space=pl.ANY)] * 7,
        scratch_shapes=[
            vmem((240, D), f32), vmem((240, D), f32), vmem((240, D), f32),
            vmem((240, RANK), f32), vmem((D, COLS), f32), vmem((D, COLS), f32),
            vmem((4, ROWS), f32), vmem((4, ROWS), f32),
            vmem((N, 4, ROWS), f32),
            vmem((N, N, D), f32), vmem((N, N, D), f32),
            vmem((N, 1, D), f32), vmem((N, 1, D), f32),
            vmem((1, 1, D), f32), vmem((N, 1, D), f32),
            vmem((1, 1, D), f32), vmem((N, 1, D), f32),
            vmem((1, N, D), f32), vmem((N, N, D), f32),
            vmem((N, ROWS, WIDE), f32),
            vmem((N, 2, ROWS, COLS), f32), vmem((N, 2, ROWS, COLS), f32),
            vmem((N, ROWS, COLS), f32), vmem((N, ROWS, COLS), f32),
            vmem((1, ROWS, WIDE), f32), vmem((N, ROWS, WIDE), f32),
            vmem((1, ROWS, WIDE), jnp.bfloat16), vmem((N, ROWS, WIDE), jnp.bfloat16),
            *[vmem(*shape) for shape in shapes],
            pltpu.SemaphoreType.DMA((11,)), pltpu.SemaphoreType.DMA((11,)),
            pltpu.SemaphoreType.DMA((2,)), pltpu.SemaphoreType.DMA((16,)),
        ],
        compiler_params=pltpu.CompilerParams(
            collective_id=0, has_side_effects=True, vmem_limit_bytes=24 << 20
        ),
    )(*args)


def solution(mesh):
    return jax.shard_map(
        on_device,
        mesh=mesh,
        in_specs=(
            P("group", "shard", None),
            P("shard", None),
            P("shard", None),
            P("shard", None),
            P("group", "shard", None),
            P(None, "shard"),
            P(None, "shard"),
            P("group", None, "shard"),
            P(None, "shard"),
            P(None, "shard"),
        ),
        out_specs=(
            P("shard", None),
            P("shard", None),
            P(None, "shard"),
            P(None, "shard"),
            P(None, "shard"),
            P(None, "shard"),
            P("shard", None),
        ),
        check_vma=False,
    )
```

time: 639 us -> 89.5 us (0.14)
  waiting for transfers between devices: 540 us -> 0 us
  Pallas kernels: 0 us -> 73.6 us
  starting transfers between devices: 38.6 us -> 0 us
  blocking collectives: 27.7 us -> 0 us
  between operations: 14.2 us -> 0.76 us
  local copies, waits for them, and re-layouts: 8.4 us -> 14.9 us
    psum x2 -> x0, waiting for transfers between devices: 523 us -> none  [the longest x1 442 us: on_device(): coeff_sum = lax.psum(partial_coeff, ('group', 'shard'))]
    pallas_call x0 -> x1, Pallas kernels: none -> 73.6 us  [on_device(): pl.pallas_call(kernel, out_shape=[jax.ShapeDtypeStruct(*shape) for shape...]
    all_to_all x2 -> x0, starting transfers between devices: 38.5 us -> none  [the longest x1 22.4 us: on_device(): lax.all_to_all(inner_attn[0], 'shard', split_axis=1, concat_axis=0, tiled...]
    psum x1 -> x0, blocking collectives: 27.7 us -> none  [on_device(): attn_sum, norm_sum = lax.psum((attn_term, norm_diff), 'group')]
    all_to_all x2 -> x0, waiting for transfers between devices: 17.3 us -> none  [the longest x1 17.3 us: on_device(): lax.all_to_all(inner_attn[0], 'shard', split_axis=1, concat_axis=0, tiled...]
  transfers between devices with their start and end apart: 4 -> 0, of which waited for: 3 -> 0; matrix products, arithmetic and copies ran while one was open for 1% -> 0% of each run, Pallas kernels for 0% -> 0%
where the time goes in v1:
time: 89.5 us; the launch traced here: 89.2 us
  Pallas kernels  73.6 us (82%)
  local copies, waits for them, and re-layouts  14.9 us (17%)
    pallas_call x1, Pallas kernels, on_device(): pl.pallas_call(kernel, out_shape=[jax.ShapeDtypeStruct(*shape) for shape...  73.6 us
    unnamed x29, local copies, waits for them, and re-layouts  11.2 us
    pallas_call x2, local copies, waits for them, and re-layouts, on_device(): pl.pallas_call(kernel, out_shape=[jax.ShapeDtypeStruct(*shape) for shape...  3.68 us

profile of v1, /device:TPU:1, one launch (start us, length us, event | category | flops | bytes accessed | tf_op | source)
XLA Modules:
  0.0 89.2 jit_solution(710425141765921401)
XLA Ops:
  0.6 0.0 copy-start.1
  0.6 1.0 %copy.17.basis = f32[240,64]{1,0:T(8,128)S(1)} copy(f32[240,64]{0,1:T(8,128)} %param.13) | data formatting | bytes 122880 | tf_op args[3]
  1.6 0.0 copy-start
  1.7 1.0 %copy.18.inner_a = f32[1,12,3072]{2,1,0:T(8,128)S(1)} copy(f32[1,12,3072]{2,0,1:T(1,128)} %param.14) | data formatting | bytes 294912 | tf_op args[4]
  2.7 1.1 %copy.19.outer_a = f32[768,48]{1,0:T(8,128)S(1)} copy(f32[768,48]{0,1:T(8,128)} %param.15) | data formatting | bytes 294912 | tf_op args[5]
  3.8 0.0 copy-start.7
  3.8 0.0 copy-start.8
  3.8 0.0 copy-start.9
  3.8 1.1 %copy.20.mom_a = f32[768,48]{1,0:T(8,128)S(1)} copy(f32[768,48]{0,1:T(8,128)} %param.16) | data formatting | bytes 294912 | tf_op args[6]
  4.9 0.0 copy-done.1
  4.9 0.0 copy-done
  4.9 0.0 copy-done.7
  4.9 0.0 copy-done.8
  4.9 0.0 copy-done.9
  4.9 0.0 copy-start.2
  4.9 1.1 %copy-done.2 = f32[240,768]{1,0:T(8,128)S(1)} copy-done((f32[240,768]{1,0:T(8,128)S(1)}, f32[240,768]{1,0:T(8,128)}, u32[]{:S(2)}) %copy-start.2) | copy-done | bytes 737304
  6.1 73.6 %shard_map.153 = (f32[240,768]{1,0:T(8,128)S(1)}, f32[240,768]{1,0:T(8,128)S(1)}, f32[768,48]{1,0:T(8,128)S(1)}, f32[768,48]{1,0:T(8,128)S(1)}, f32[4,12]{1,0:T(...) custom-call(f32[1,240,768]{2,1,0:T(8,128)S(1)} %copy-done, f32[240,768]{1,0:T(8,128)S(1)} %copy-done.1, ...), custom_call_target="tpu_custom_call" | custom-call | tf_op jit(solution)/shard_map/pallas_call | solution.py:289
  79.6 0.0 copy-start.3
  79.6 0.9 copy-done.3
  80.5 0.0 copy-start.5
  80.5 0.7 copy-done.5
  81.2 0.0 copy-start.6
  81.2 0.7 copy-done.6
  82.0 0.0 copy-start.4
  82.0 1.9 %copy.21 = f32[768,48]{0,1:T(8,128)} copy(f32[768,48]{1,0:T(8,128)} %copy-done.6) | data formatting | bytes 294912 | tf_op jit(solution)/shard_map/pallas_call | solution.py:289
  83.8 1.8 %copy.22 = f32[768,48]{0,1:T(8,128)} copy(f32[768,48]{1,0:T(8,128)} %copy-done.5) | data formatting | bytes 294912 | tf_op jit(solution)/shard_map/pallas_call | solution.py:289
  85.6 0.0 copy-done.4
  85.7 0.9 copy.28
  86.5 0.9 copy.29
  87.4 0.6 copy.30
  88.0 0.6 copy.31
  88.5 0.6 copy.32
Async XLA Ops:
  0.6 4.3 %copy-start.1 = (f32[240,768]{1,0:T(8,128)S(1)}, f32[240,768]{1,0:T(8,128)}, u32[]{:S(2)}) copy-start(f32[240,768]{1,0:T(8,128)} %outer_e.1) | copy-start | bytes 2211844
  1.6 3.2 %copy-start = (f32[1,240,768]{2,1,0:T(8,128)S(1)}, f32[1,240,768]{2,1,0:T(8,128)}, u32[]{:S(2)}) copy-start(f32[1,240,768]{2,1,0:T(8,128)} %inner_e.1) | copy-start | bytes 2211844
  3.8 1.1 %copy-start.7 = (f32[1,4,12]{2,1,0:T(4,128)S(1)}, f32[1,4,12]{2,1,0:T(4,128)}, u32[]{:S(2)}) copy-start(f32[1,4,12]{2,1,0:T(4,128)} %inner_n.1) | copy-start | bytes 580
  3.8 1.1 %copy-start.8 = (f32[4,12]{1,0:T(4,128)S(1)}, f32[4,12]{1,0:T(4,128)}, u32[]{:S(2)}) copy-start(f32[4,12]{1,0:T(4,128)} %outer_n.1) | copy-start | bytes 580
  3.8 1.1 %copy-start.9 = (f32[4,12]{1,0:T(4,128)S(1)}, f32[4,12]{1,0:T(4,128)}, u32[]{:S(2)}) copy-start(f32[4,12]{1,0:T(4,128)} %mom_n.1) | copy-start | bytes 580
  4.9 1.1 %copy-start.2 = (f32[240,768]{1,0:T(8,128)S(1)}, f32[240,768]{1,0:T(8,128)}, u32[]{:S(2)}) copy-start(f32[240,768]{1,0:T(8,128)} %mom_e.1) | copy-start | bytes 2211844
  79.6 0.9 copy-start.3
  80.5 0.7 copy-start.5
  81.2 0.7 copy-start.6
  82.0 3.7 %copy-start.4 = (f32[240,768]{1,0:T(8,128)S(1)}, f32[240,768]{1,0:T(8,128)}, u32[]{:S(2)}) copy-start(f32[240,768]{1,0:T(8,128)} %copy-done.3) | copy-start | bytes 2211844

commit v2 on v1

v2 whole, which is shorter than its diff:
```python
import math

import jax
import jax.numpy as jnp
from jax import lax
from jax.experimental import pallas as pl
from jax.experimental.pallas import tpu as pltpu
from jax.sharding import PartitionSpec as P

VOCAB = 15360
RANK = 64
D = 768
N = 8
PLANE = 32
RING = 16
ROWS = 12
COLS = 48
WIDE = N * COLS
TALL = N * ROWS
PAIR = RANK // PLANE
MESH = pl.DeviceIdType.MESH
HIGHEST = lax.Precision.HIGHEST
SCALE = 1.0 / math.sqrt(RANK * VOCAB)
F32 = jnp.float32
BF16 = jnp.bfloat16

C1, CZ, C3, P1, W, NR, SW, AG, RP = range(9)
L_IE, L_OE, L_BA, L_OA, L_MA, L_IA, L_IN, L_ON = range(8)

G_STEPS = (4, 5, 3, 6, 2, 7, 1)
Z_STEPS = tuple(sorted(range(1, RING), key=lambda k: -min(k, RING - k)))
P_STEPS = tuple(
    sorted(
        [(i, j, k) for i in range(4) for j in range(4) for k in range(2)][1:],
        key=lambda t: -(min(t[0], 4 - t[0]) + min(t[1], 4 - t[1])),
    )
)


def nesterov(outer, moment, delta):
    moment_new = 0.5 * moment + delta
    return (outer - (delta + 0.5 * moment_new), moment_new)


def across(g, b):
    half, x = b // 4, lax.rem(b, 4)
    inner = jnp.logical_and(g >= 2, g <= 5)
    low = jnp.where(half == 0, g, 7 - g)
    outer_turn = jnp.where(low < 2, low, low - 4)
    turn = jnp.where(inner, g - 2, outer_turn)
    high, bit = turn // 2, lax.rem(turn, 2)
    x_high, x_bit = x // 2, lax.rem(x, 2)
    moved = 2 * lax.rem(x_high + high, 2) + lax.rem(x_bit + bit, 2)
    return (
        jnp.where(inner, g, 7 - g),
        4 * jnp.where(inner, half, 1 - half) + moved,
    )


def exchange(
    inner_e, outer_e, basis, inner_a, outer_a, mom_a, inner_n, outer_n,
    coef, delta_t, rep, norm,
    v_ie, v_oe, v_ba, v_oa, v_ma, v_on,
    c_part, r_c1, c_own, r_cz, c_fin, r_c3,
    r_p1, w_out, r_w, d_out, r_d, d_all, r_ag, rp_out, r_rp, r_norm,
    send, recv, once, local,
):
    g = lax.axis_index("group")
    s = lax.axis_index("shard")
    b, a = s // N, lax.rem(s, N)
    half, p = s // PLANE, lax.rem(s, PLANE)
    x, y, core = p // 8, lax.rem(p // 2, 4), lax.rem(p, 2)
    z = N * half + g
    far_g, far_b = across(g, b)

    def in_plane(step):
        i, j, k = step
        return 8 * lax.rem(x + i, 4) + 2 * lax.rem(y + j, 4) + lax.rem(core + k, 2)

    plane = [in_plane(step) for step in P_STEPS]
    ring = [lax.rem(z + k, RING) for k in Z_STEPS]
    line = [lax.rem(g + k, N) for k in G_STEPS]
    turns = [lax.rem(a + k, N) for k in range(N)]
    to_plane = [(g, PLANE * half + q) for q in plane]
    to_ring = [(lax.rem(q, N), PLANE * (q // N) + p) for q in ring]
    to_line = [(q, s) for q in line]
    to_swap = [(far_g, N * far_b + q) for q in turns]
    crossing = jnp.logical_or(far_b != b, far_g != g)

    def load(src, dst, sem):
        copy = pltpu.make_async_copy(src, dst, local.at[sem])
        copy.start()
        return copy

    def block(q):
        return inner_a.at[:, :, pl.ds(pl.multiple_of(q * WIDE, 128), WIDE)]

    ld_oa = load(outer_a, v_oa, L_OA)
    ld_ma = load(mom_a, v_ma, L_MA)
    ld_ie = load(inner_e.at[0], v_ie, L_IE)
    ld_oe = load(outer_e, v_oe, L_OE)
    ld_ba = load(basis, v_ba, L_BA)
    ld_ia = load(block(far_b), r_p1.at[g], L_IA)
    ld_in = load(inner_n.at[0], r_norm.at[g], L_IN)
    ld_on = load(outer_n, v_on, L_ON)

    barrier = pltpu.get_barrier_semaphore()

    def greet(device):
        pl.semaphore_signal(barrier, inc=1, device_id=device, device_id_type=MESH)

    for device in to_ring + to_plane + to_swap[1:]:
        greet(device)

    @pl.when(crossing)
    def _():
        greet(to_swap[0])

    def put(src, dst, phase, device, send_sem=None):
        pltpu.make_async_remote_copy(
            src_ref=src,
            dst_ref=dst,
            send_sem=send.at[phase] if send_sem is None else send_sem,
            recv_sem=recv.at[phase],
            device_id=device,
            device_id_type=MESH,
        ).start()

    def whole(ref, phase, count):
        part = ref.at[pl.ds(0, count)]
        return pltpu.make_async_remote_copy(
            src_ref=part,
            dst_ref=part,
            send_sem=send.at[phase],
            recv_sem=recv.at[phase],
            device_id=to_line[0],
            device_id_type=MESH,
        )

    def arrived(ref, phase):
        whole(ref, phase, ref.shape[0] - 1).wait_recv()

    def swap(src, dst, phase, turn):
        for k in range(1, N):
            put(src.at[turns[k]], dst.at[a], phase, to_swap[k])

        @pl.when(crossing)
        def _():
            put(src.at[a], dst.at[a], phase, to_swap[0], once.at[turn])

        @pl.when(jnp.logical_not(crossing))
        def _():
            dst[a] = src[a]

    def swap_arrived(ref, phase):
        @pl.when(crossing)
        def _():
            whole(ref, phase, N).wait_recv()

        @pl.when(jnp.logical_not(crossing))
        def _():
            whole(ref, phase, N - 1).wait_recv()

    ld_ie.wait()
    ld_oe.wait()
    ld_ba.wait()
    part = jnp.dot(
        v_ba[...],
        v_oe[...] - v_ie[...],
        precision=HIGHEST,
        preferred_element_type=F32,
    )
    for j in range(PLANE):
        c_part[j] = part[PAIR * j : PAIR * (j + 1), :]

    ld_oa.wait()
    ld_ma.wait()
    for i, ref in enumerate((v_oa, v_ma)):
        state = ref[...]
        rows = state[:, :TALL]
        for j in range(1, N):
            rows = jnp.where(far_b == j, state[:, TALL * j : TALL * (j + 1)], rows)
        rows = rows.T
        for j in range(N):
            w_out[j, i] = rows[ROWS * j : ROWS * (j + 1), :]

    pl.semaphore_wait(
        barrier, RING - 1 + PLANE - 1 + N - 1 + jnp.where(crossing, 1, 0)
    )

    for q, device in zip(plane, to_plane):
        put(c_part.at[q], r_c1.at[p], C1, device)
    for q, device in zip(line, to_line):
        put(block(across(q, b)[1]), r_p1.at[g], P1, device)
    swap(w_out, r_w, W, 0)
    for device in to_line:
        put(inner_n.at[0], r_norm.at[g], NR, device)

    r_c1[p] = c_part[p]
    arrived(r_c1, C1)
    row = r_c1[0]
    for j in range(1, PLANE):
        row = row + r_c1[j]
    c_own[0] = row
    for device in to_ring:
        put(c_own.at[0], r_cz.at[z], CZ, device)
    r_cz[z] = row

    swap_arrived(r_w, W)
    outer_wide = jnp.concatenate([r_w[j, 0] for j in range(N)], axis=1)
    mom_wide = jnp.concatenate([r_w[j, 1] for j in range(N)], axis=1)
    ld_ia.wait()
    arrived(r_p1, P1)
    total = outer_wide - r_p1[0, :, 0, :]
    for j in range(1, N):
        total = total + (outer_wide - r_p1[j, :, 0, :])
    delta = total * (1.0 / N)
    for j in range(N):
        d_out[j] = delta[:, COLS * j : COLS * (j + 1)]
    swap(d_out, r_d, SW, 1)
    replica = nesterov(outer_wide, mom_wide, delta)[0].astype(BF16)
    rp_out[0] = replica
    for device in to_line:
        put(rp_out.at[0], r_rp.at[far_b], RP, device)
    r_rp[far_b] = replica

    swap_arrived(r_d, SW)
    tall = jnp.concatenate([r_d[j] for j in range(N)], axis=0).T
    d_all[0] = tall
    for device in to_line:
        put(d_all.at[0], r_ag.at[far_b], AG, device)
    r_ag[far_b] = tall

    arrived(r_cz, CZ)
    row = r_cz[0]
    for j in range(1, RING):
        row = row + r_cz[j]
    row = row * (1.0 / N)
    c_fin[0] = row
    for device in to_plane:
        put(c_fin.at[0], r_c3.at[p], C3, device)
    r_c3[p] = row

    ld_in.wait()
    ld_on.wait()
    arrived(r_norm, NR)
    outer_norm = v_on[...]
    total = outer_norm - r_norm[0]
    for j in range(1, N):
        total = total + (outer_norm - r_norm[j])
    norm[...] = total * (1.0 / N)

    arrived(r_rp, RP)
    for j in range(N):
        rep[:, WIDE * j : WIDE * (j + 1)] = r_rp[j]
    arrived(r_c3, C3)
    for j in range(PLANE):
        coef[PAIR * j : PAIR * (j + 1), :] = r_c3[j]
    arrived(r_ag, AG)
    for j in range(N):
        delta_t[:, TALL * j : TALL * (j + 1)] = r_ag[j]

    for ref, phase in (
        (r_c1, C1), (r_cz, CZ), (r_c3, C3), (r_p1, P1), (r_norm, NR), (r_ag, AG),
        (r_rp, RP),
    ):
        whole(ref, phase, ref.shape[0] - 1).wait_send()
    for ref, phase in ((r_w, W), (r_d, SW)):
        whole(ref, phase, N - 1).wait_send()

    @pl.when(crossing)
    def _():
        for ref, turn in ((r_w, 0), (r_d, 1)):
            pltpu.make_async_remote_copy(
                src_ref=ref.at[0],
                dst_ref=ref.at[0],
                send_sem=once.at[turn],
                recv_sem=recv.at[W],
                device_id=to_line[0],
                device_id_type=MESH,
            ).wait_send()


def finish(
    coef, delta_t, rep, norm, outer_e, mom_e, basis, outer_a, mom_a, outer_n, mom_n,
    new_e, new_me, new_a, new_ma, new_n, new_mn, new_rep,
    o_e, o_me, o_a, o_ma, o_n, o_mn, sems,
):
    copies = []

    def store(src, dst):
        copy = pltpu.make_async_copy(src, dst, sems.at[len(copies)])
        copy.start()
        copies.append(copy)

    store(rep, new_rep)
    change = lax.dot_general(
        basis[...],
        coef[...],
        (((0,), (0,)), ((), ())),
        precision=HIGHEST,
        preferred_element_type=F32,
    ) * SCALE
    o_e[...], o_me[...] = nesterov(outer_e[...], mom_e[...], change)
    store(o_e, new_e)
    store(o_me, new_me)
    o_a[...], o_ma[...] = nesterov(outer_a[...], mom_a[...], delta_t[...])
    store(o_a, new_a)
    store(o_ma, new_ma)
    o_n[...], o_mn[...] = nesterov(outer_n[...], mom_n[...], norm[...])
    store(o_n, new_n)
    store(o_mn, new_mn)
    for copy in copies:
        copy.wait()


def on_device(
    inner_embed, outer_embed, moment_embed, basis, inner_attn, outer_attn,
    moment_attn, inner_norms, outer_norms, moment_norms,
):
    vmem = pltpu.VMEM
    dma = pltpu.SemaphoreType.DMA
    basis_t, outer_t, moment_t = basis.T, outer_attn.T, moment_attn.T
    inner_rows = inner_attn.reshape(ROWS, 1, 4 * D)
    in_place = pl.BlockSpec(memory_space=pl.ANY)
    on_chip = pl.BlockSpec(memory_space=pltpu.VMEM)
    shape = jax.ShapeDtypeStruct
    vocab = outer_embed.shape[0]

    coef, delta_t, rep, norm = pl.pallas_call(
        exchange,
        out_shape=[
            shape((RANK, D), F32), shape((COLS, D), F32),
            shape((ROWS, 4 * D), BF16), shape((4, ROWS), F32),
        ],
        in_specs=[in_place] * 8,
        out_specs=[on_chip] * 4,
        scratch_shapes=[
            vmem((vocab, D), F32), vmem((vocab, D), F32), vmem((RANK, vocab), F32),
            vmem((COLS, D), F32), vmem((COLS, D), F32), vmem((4, ROWS), F32),
            vmem((PLANE, PAIR, D), F32), vmem((PLANE, PAIR, D), F32),
            vmem((1, PAIR, D), F32), vmem((RING, PAIR, D), F32),
            vmem((1, PAIR, D), F32), vmem((PLANE, PAIR, D), F32),
            vmem((N, ROWS, 1, WIDE), F32),
            vmem((N, 2, ROWS, COLS), F32), vmem((N, 2, ROWS, COLS), F32),
            vmem((N, ROWS, COLS), F32), vmem((N, ROWS, COLS), F32),
            vmem((1, COLS, TALL), F32), vmem((N, COLS, TALL), F32),
            vmem((1, ROWS, WIDE), BF16), vmem((N, ROWS, WIDE), BF16),
            vmem((N, 4, ROWS), F32),
            dma((9,)), dma((9,)), dma((2,)), dma((8,)),
        ],
        compiler_params=pltpu.CompilerParams(
            collective_id=0, has_side_effects=True, vmem_limit_bytes=24 << 20
        ),
    )(
        inner_embed, outer_embed, basis_t, inner_rows, outer_t, moment_t,
        inner_norms, outer_norms,
    )

    outs = [
        shape((vocab, D), F32), shape((vocab, D), F32), shape((COLS, D), F32),
        shape((COLS, D), F32), shape((4, ROWS), F32), shape((4, ROWS), F32),
    ]
    new_e, new_me, new_a, new_ma, new_n, new_mn, replica = pl.pallas_call(
        finish,
        out_shape=[*outs, shape((ROWS, 4 * D), BF16)],
        in_specs=[on_chip] * 11,
        out_specs=[in_place] * 7,
        scratch_shapes=[*[vmem(out.shape, F32) for out in outs], dma((7,))],
        compiler_params=pltpu.CompilerParams(vmem_limit_bytes=16 << 20),
    )(
        coef, delta_t, rep, norm, outer_embed, moment_embed, basis_t, outer_t,
        moment_t, outer_norms, moment_norms,
    )
    return new_e, new_me, new_a.T, new_ma.T, new_n, new_mn, replica


def solution(mesh):
    return jax.shard_map(
        on_device,
        mesh=mesh,
        in_specs=(
            P("group", "shard", None),
            P("shard", None),
            P("shard", None),
            P("shard", None),
            P("group", "shard", None),
            P(None, "shard"),
            P(None, "shard"),
            P("group", None, "shard"),
            P(None, "shard"),
            P(None, "shard"),
        ),
        out_specs=(
            P("shard", None),
            P("shard", None),
            P(None, "shard"),
            P(None, "shard"),
            P(None, "shard"),
            P(None, "shard"),
            P("shard", None),
        ),
        check_vma=False,
    )
```

time: 89.5 us -> 56.9 us (0.64)
  Pallas kernels: 73.6 us -> 48.7 us
  local copies, waits for them, and re-layouts: 14.9 us -> 7.15 us
    pallas_call x1 -> x2, Pallas kernels: 73.6 us -> 48.7 us  [the longest x1 46.6 us: on_device(): pl.pallas_call(exchange, out_shape=[shape((RANK, D), F32), shape((COLS, D...]
    unnamed x29 -> x20, local copies, waits for them, and re-layouts: 11.2 us -> 7.15 us
    pallas_call x2 -> x0, local copies, waits for them, and re-layouts: 3.68 us -> none  [on_device(): pl.pallas_call(kernel, out_shape=[jax.ShapeDtypeStruct(*shape) for shape...]
where the time goes in v2:
time: 56.9 us; the launch traced here: 56.5 us
  Pallas kernels  48.7 us (86%)
  local copies, waits for them, and re-layouts  7.15 us (13%)
  between operations  0.68 us (1%)
    pallas_call x1, Pallas kernels, on_device(): pl.pallas_call(exchange, out_shape=[shape((RANK, D), F32), shape((COLS, D...  46.6 us
    unnamed x20, local copies, waits for them, and re-layouts  7.15 us
    pallas_call x1, Pallas kernels, on_device(): pl.pallas_call(finish, out_shape=[*outs, shape((ROWS, 4 * D), BF16)], in_...  2.1 us

profile of v2, /device:TPU:1, one launch (start us, length us, event | category | flops | bytes accessed | tf_op | source)
XLA Modules:
  0.0 56.5 jit_solution(16695325683596270622)
XLA Ops:
  0.6 0.0 copy-start.8
  0.6 0.0 copy-start.7
  0.7 0.7 %copy-done.8 = f32[1,4,12]{2,1,0:T(4,128)S(1)} copy-done((f32[1,4,12]{2,1,0:T(4,128)S(1)}, f32[1,4,12]{2,1,0:T(4,128)}, u32[]{:S(2)}) %copy-start.8) | copy-done | bytes 216
  1.3 0.0 copy-done.7
  1.3 0.0 copy-start
  1.3 1.1 %copy-done = f32[240,768]{1,0:T(8,128)S(1)} copy-done((f32[240,768]{1,0:T(8,128)S(1)}, f32[240,768]{1,0:T(8,128)}, u32[]{:S(2)}) %copy-start) | copy-done | bytes 737304
  2.5 0.0 copy-start.2
  2.5 1.1 %copy-done.2 = f32[1,240,768]{2,1,0:T(8,128)S(1)} copy-done((f32[1,240,768]{2,1,0:T(8,128)S(1)}, f32[1,240,768]{2,1,0:T(8,128)}, u32[]{:S(2)}) %copy-start.2) | copy-done | bytes 737304
  3.6 0.0 copy-start.3
  3.6 0.9 %copy-done.3 = f32[768,48]{0,1:T(8,128)S(1)} copy-done((f32[768,48]{0,1:T(8,128)S(1)}, f32[768,48]{0,1:T(8,128)}, u32[]{:S(2)}) %copy-start.3) | copy-done | bytes 147480
  4.5 0.0 copy-start.4
  4.5 0.9 %copy-done.4 = f32[768,48]{0,1:T(8,128)S(1)} copy-done((f32[768,48]{0,1:T(8,128)S(1)}, f32[768,48]{0,1:T(8,128)}, u32[]{:S(2)}) %copy-start.4) | copy-done | bytes 147480
  5.4 0.0 copy-start.5
  5.4 0.8 %copy-done.5 = f32[240,64]{0,1:T(8,128)S(1)} copy-done((f32[240,64]{0,1:T(8,128)S(1)}, f32[240,64]{0,1:T(8,128)}, u32[]{:S(2)}) %copy-start.5) | copy-done | bytes 61464
  6.2 0.0 copy-start.6
  6.2 0.9 %copy-done.6 = f32[1,12,3072]{2,0,1:T(1,128)S(1)} copy-done((f32[1,12,3072]{2,0,1:T(1,128)S(1)}, f32[1,12,3072]{2,0,1:T(1,128)}, u32[]{:S(2)}) %copy-start.6) | copy-done | bytes 147480
  7.1 0.0 copy-start.1
  7.1 46.6 %shard_map.153 = (f32[64,768]{1,0:T(8,128)S(1)}, f32[48,768]{1,0:T(8,128)S(1)}, bf16[12,3072]{1,0:T(8,128)(2,1)S(1)}, f32[4,12]{1,0:T(4,128)S(1)}) custom-call(f32[1,240,768]{2,1,0:T(8,128)S(1)} %copy-done.2, f32[240,768]{1,0:T(8,128)S(1)} %copy-done, f32[64,240]{1,0:T(8,128)S(1)} %bitcast.10, f32[12,1,3072]{2,1,0:T(1,128)S(1)} %bitcast.12, ...), custom_call_target="tpu_custom_call" | custom-call | tf_op jit(solution)/shard_map/pallas_call | solution.py:330
  53.7 0.0 copy-start.9
  53.8 0.0 copy-done.1
  53.8 0.7 %copy-done.9 = f32[4,12]{1,0:T(4,128)S(1)} copy-done((f32[4,12]{1,0:T(4,128)S(1)}, f32[4,12]{1,0:T(4,128)}, u32[]{:S(2)}) %copy-start.9) | copy-done | bytes 216
  54.4 2.1 %shard_map.154 = (f32[240,768]{1,0:T(8,128)}, f32[240,768]{1,0:T(8,128)}, f32[48,768]{1,0:T(8,128)}, f32[48,768]{1,0:T(8,128)}, f32[4,12]{1,0:T(4,128)}, /*index=5*/f32[4,12]{1,0:T(4,128)}, bf16[12,3072]{1,0:T(8,128)(2,1)}) custom-call(f32[64,768]{1,0:T(8,128)S(1)} %get-tuple-element.18.coef, f32[48,768]{1,0:T(8,128)S(1)} %get-tuple-element.19.delta_t, ...), custom_call_target="tpu_custom_call" | custom-call | tf_op jit(solution)/shard_map/pallas_call | solution.py:364
Async XLA Ops:
  0.6 0.7 %copy-start.8 = (f32[1,4,12]{2,1,0:T(4,128)S(1)}, f32[1,4,12]{2,1,0:T(4,128)}, u32[]{:S(2)}) copy-start(f32[1,4,12]{2,1,0:T(4,128)} %inner_n.1) | copy-start | bytes 580
  0.6 0.7 %copy-start.7 = (f32[4,12]{1,0:T(4,128)S(1)}, f32[4,12]{1,0:T(4,128)}, u32[]{:S(2)}) copy-start(f32[4,12]{1,0:T(4,128)} %outer_n.3) | copy-start | bytes 580
  1.3 1.1 %copy-start = (f32[240,768]{1,0:T(8,128)S(1)}, f32[240,768]{1,0:T(8,128)}, u32[]{:S(2)}) copy-start(f32[240,768]{1,0:T(8,128)} %outer_e.3) | copy-start | bytes 2211844
  2.5 1.1 %copy-start.2 = (f32[1,240,768]{2,1,0:T(8,128)S(1)}, f32[1,240,768]{2,1,0:T(8,128)}, u32[]{:S(2)}) copy-start(f32[1,240,768]{2,1,0:T(8,128)} %inner_e.1) | copy-start | bytes 2211844
  3.6 0.9 %copy-start.3 = (f32[768,48]{0,1:T(8,128)S(1)}, f32[768,48]{0,1:T(8,128)}, u32[]{:S(2)}) copy-start(f32[768,48]{0,1:T(8,128)} %param.15) | copy-start | bytes 442372
  4.5 0.9 %copy-start.4 = (f32[768,48]{0,1:T(8,128)S(1)}, f32[768,48]{0,1:T(8,128)}, u32[]{:S(2)}) copy-start(f32[768,48]{0,1:T(8,128)} %param.16) | copy-start | bytes 442372
  5.4 0.8 %copy-start.5 = (f32[240,64]{0,1:T(8,128)S(1)}, f32[240,64]{0,1:T(8,128)}, u32[]{:S(2)}) copy-start(f32[240,64]{0,1:T(8,128)} %param.13) | copy-start | bytes 184324
  6.2 0.9 %copy-start.6 = (f32[1,12,3072]{2,0,1:T(1,128)S(1)}, f32[1,12,3072]{2,0,1:T(1,128)}, u32[]{:S(2)}) copy-start(f32[1,12,3072]{2,0,1:T(1,128)} %param.14) | copy-start | bytes 442372
  7.1 46.6 %copy-start.1 = (f32[240,768]{1,0:T(8,128)S(1)}, f32[240,768]{1,0:T(8,128)}, u32[]{:S(2)}) copy-start(f32[240,768]{1,0:T(8,128)} %mom_e.1) | copy-start | bytes 2211844
  53.7 0.7 %copy-start.9 = (f32[4,12]{1,0:T(4,128)S(1)}, f32[4,12]{1,0:T(4,128)}, u32[]{:S(2)}) copy-start(f32[4,12]{1,0:T(4,128)} %mom_n.1) | copy-start | bytes 580

commit v3 on v2

--- a/solution.py
+++ b/solution.py
@@ -25,7 +25,7 @@
 BF16 = jnp.bfloat16
 
 C1, CZ, C3, P1, W, NR, SW, AG, RP = range(9)
-L_IE, L_OE, L_BA, L_OA, L_MA, L_IA, L_IN, L_ON = range(8)
+L_IE, L_OE, L_ME, L_BA, L_OA, L_MA, L_IA, L_IN, L_ON, L_MN = range(10)
 
 G_STEPS = (4, 5, 3, 6, 2, 7, 1)
 Z_STEPS = tuple(sorted(range(1, RING), key=lambda k: -min(k, RING - k)))
@@ -58,11 +58,11 @@
 
 
 def exchange(
-    inner_e, outer_e, basis, inner_a, outer_a, mom_a, inner_n, outer_n,
-    coef, delta_t, rep, norm,
-    v_ie, v_oe, v_ba, v_oa, v_ma, v_on,
-    c_part, r_c1, c_own, r_cz, c_fin, r_c3,
-    r_p1, w_out, r_w, d_out, r_d, d_all, r_ag, rp_out, r_rp, r_norm,
+    inner_e, outer_e, mom_e, basis, inner_a, outer_a, mom_a, inner_n, outer_n, mom_n,
+    o_e, o_me, o_a, o_ma, o_n, o_mn, rep,
+    v_ie, v_oe, v_me, v_ba, v_oa, v_ma, v_on, v_mn,
+    c_part, r_c1, c_own, r_cz, c_fin, r_c3, coef,
+    r_p1, w_out, r_w, d_out, r_d, d_all, r_ag, delta_t, rp_out, r_rp, r_norm,
     send, recv, once, local,
 ):
     g = lax.axis_index("group")
@@ -87,6 +87,18 @@
     to_swap = [(far_g, N * far_b + q) for q in turns]
     crossing = jnp.logical_or(far_b != b, far_g != g)
 
+    barrier = pltpu.get_barrier_semaphore()
+
+    def greet(device):
+        pl.semaphore_signal(barrier, inc=1, device_id=device, device_id_type=MESH)
+
+    for device in to_ring + to_plane + to_swap[1:]:
+        greet(device)
+
+    @pl.when(crossing)
+    def _():
+        greet(to_swap[0])
+
     def load(src, dst, sem):
         copy = pltpu.make_async_copy(src, dst, local.at[sem])
         copy.start()
@@ -103,18 +115,8 @@
     ld_ia = load(block(far_b), r_p1.at[g], L_IA)
     ld_in = load(inner_n.at[0], r_norm.at[g], L_IN)
     ld_on = load(outer_n, v_on, L_ON)
-
-    barrier = pltpu.get_barrier_semaphore()
-
-    def greet(device):
-        pl.semaphore_signal(barrier, inc=1, device_id=device, device_id_type=MESH)
-
-    for device in to_ring + to_plane + to_swap[1:]:
-        greet(device)
-
-    @pl.when(crossing)
-    def _():
-        greet(to_swap[0])
+    ld_mn = load(mom_n, v_mn, L_MN)
+    ld_me = load(mom_e, v_me, L_ME)
 
     def put(src, dst, phase, device, send_sem=None):
         pltpu.make_async_remote_copy(
@@ -161,17 +163,12 @@
         def _():
             whole(ref, phase, N - 1).wait_recv()
 
-    ld_ie.wait()
-    ld_oe.wait()
-    ld_ba.wait()
-    part = jnp.dot(
-        v_ba[...],
-        v_oe[...] - v_ie[...],
-        precision=HIGHEST,
-        preferred_element_type=F32,
-    )
-    for j in range(PLANE):
-        c_part[j] = part[PAIR * j : PAIR * (j + 1), :]
+    pl.semaphore_wait(
+        barrier, RING - 1 + PLANE - 1 + N - 1 + jnp.where(crossing, 1, 0)
+    )
+
+    for q, device in zip(line, to_line):
+        put(block(across(q, b)[1]), r_p1.at[g], P1, device)
 
     ld_oa.wait()
     ld_ma.wait()
@@ -183,20 +180,28 @@
         rows = rows.T
         for j in range(N):
             w_out[j, i] = rows[ROWS * j : ROWS * (j + 1), :]
-
-    pl.semaphore_wait(
-        barrier, RING - 1 + PLANE - 1 + N - 1 + jnp.where(crossing, 1, 0)
-    )
-
+    swap(w_out, r_w, W, 0)
+
+    ld_ie.wait()
+    ld_oe.wait()
+    ld_ba.wait()
+    part = jnp.dot(
+        v_ba[...],
+        v_oe[...] - v_ie[...],
+        precision=HIGHEST,
+        preferred_element_type=F32,
+    )
+    for j in range(PLANE):
+        c_part[j] = part[PAIR * j : PAIR * (j + 1), :]
     for q, device in zip(plane, to_plane):
         put(c_part.at[q], r_c1.at[p], C1, device)
-    for q, device in zip(line, to_line):
-        put(block(across(q, b)[1]), r_p1.at[g], P1, device)
-    swap(w_out, r_w, W, 0)
+    r_c1[p] = c_part[p]
     for device in to_line:
         put(inner_n.at[0], r_norm.at[g], NR, device)
 
-    r_c1[p] = c_part[p]
+    swap_arrived(r_w, W)
+    outer_wide = jnp.concatenate([r_w[j, 0] for j in range(N)], axis=1)
+    mom_wide = jnp.concatenate([r_w[j, 1] for j in range(N)], axis=1)
     arrived(r_c1, C1)
     row = r_c1[0]
     for j in range(1, PLANE):
@@ -205,10 +210,6 @@
     for device in to_ring:
         put(c_own.at[0], r_cz.at[z], CZ, device)
     r_cz[z] = row
-
-    swap_arrived(r_w, W)
-    outer_wide = jnp.concatenate([r_w[j, 0] for j in range(N)], axis=1)
-    mom_wide = jnp.concatenate([r_w[j, 1] for j in range(N)], axis=1)
     ld_ia.wait()
     arrived(r_p1, P1)
     total = outer_wide - r_p1[0, :, 0, :]
@@ -224,6 +225,16 @@
         put(rp_out.at[0], r_rp.at[far_b], RP, device)
     r_rp[far_b] = replica
 
+    ld_in.wait()
+    ld_on.wait()
+    ld_mn.wait()
+    arrived(r_norm, NR)
+    outer_norm = v_on[...]
+    total = outer_norm - r_norm[0]
+    for j in range(1, N):
+        total = total + (outer_norm - r_norm[j])
+    o_n[...], o_mn[...] = nesterov(outer_norm, v_mn[...], total * (1.0 / N))
+
     swap_arrived(r_d, SW)
     tall = jnp.concatenate([r_d[j] for j in range(N)], axis=0).T
     d_all[0] = tall
@@ -241,24 +252,27 @@
         put(c_fin.at[0], r_c3.at[p], C3, device)
     r_c3[p] = row
 
-    ld_in.wait()
-    ld_on.wait()
-    arrived(r_norm, NR)
-    outer_norm = v_on[...]
-    total = outer_norm - r_norm[0]
-    for j in range(1, N):
-        total = total + (outer_norm - r_norm[j])
-    norm[...] = total * (1.0 / N)
-
     arrived(r_rp, RP)
     for j in range(N):
         rep[:, WIDE * j : WIDE * (j + 1)] = r_rp[j]
+
+    ld_me.wait()
     arrived(r_c3, C3)
     for j in range(PLANE):
         coef[PAIR * j : PAIR * (j + 1), :] = r_c3[j]
+    change = lax.dot_general(
+        v_ba[...],
+        coef[...],
+        (((0,), (0,)), ((), ())),
+        precision=HIGHEST,
+        preferred_element_type=F32,
+    ) * SCALE
+    o_e[...], o_me[...] = nesterov(v_oe[...], v_me[...], change)
+
     arrived(r_ag, AG)
     for j in range(N):
         delta_t[:, TALL * j : TALL * (j + 1)] = r_ag[j]
+    o_a[...], o_ma[...] = nesterov(v_oa[...], v_ma[...], delta_t[...])
 
     for ref, phase in (
         (r_c1, C1), (r_cz, CZ), (r_c3, C3), (r_p1, P1), (r_norm, NR), (r_ag, AG),
@@ -281,35 +295,13 @@
             ).wait_send()
 
 
-def finish(
-    coef, delta_t, rep, norm, outer_e, mom_e, basis, outer_a, mom_a, outer_n, mom_n,
-    new_e, new_me, new_a, new_ma, new_n, new_mn, new_rep,
-    o_e, o_me, o_a, o_ma, o_n, o_mn, sems,
-):
-    copies = []
-
-    def store(src, dst):
-        copy = pltpu.make_async_copy(src, dst, sems.at[len(copies)])
+def write(*refs):
+    sems = refs[-1]
+    copies = [
+        pltpu.make_async_copy(refs[i], refs[7 + i], sems.at[i]) for i in range(7)
+    ]
+    for copy in copies:
         copy.start()
-        copies.append(copy)
-
-    store(rep, new_rep)
-    change = lax.dot_general(
-        basis[...],
-        coef[...],
-        (((0,), (0,)), ((), ())),
-        precision=HIGHEST,
-        preferred_element_type=F32,
-    ) * SCALE
-    o_e[...], o_me[...] = nesterov(outer_e[...], mom_e[...], change)
-    store(o_e, new_e)
-    store(o_me, new_me)
-    o_a[...], o_ma[...] = nesterov(outer_a[...], mom_a[...], delta_t[...])
-    store(o_a, new_a)
-    store(o_ma, new_ma)
-    o_n[...], o_mn[...] = nesterov(outer_n[...], mom_n[...], norm[...])
-    store(o_n, new_n)
-    store(o_mn, new_mn)
     for copy in copies:
         copy.wait()
 
@@ -323,55 +315,59 @@
     basis_t, outer_t, moment_t = basis.T, outer_attn.T, moment_attn.T
     inner_rows = inner_attn.reshape(ROWS, 1, 4 * D)
     in_place = pl.BlockSpec(memory_space=pl.ANY)
+    in_hbm = pl.BlockSpec(memory_space=pltpu.HBM)
     on_chip = pl.BlockSpec(memory_space=pltpu.VMEM)
     shape = jax.ShapeDtypeStruct
     vocab = outer_embed.shape[0]
 
-    coef, delta_t, rep, norm = pl.pallas_call(
+    outs = [
+        shape((vocab, D), F32), shape((vocab, D), F32), shape((COLS, D), F32),
+        shape((COLS, D), F32), shape((4, ROWS), F32), shape((4, ROWS), F32),
+        shape((ROWS, 4 * D), BF16),
+    ]
+    results = pl.pallas_call(
         exchange,
-        out_shape=[
-            shape((RANK, D), F32), shape((COLS, D), F32),
-            shape((ROWS, 4 * D), BF16), shape((4, ROWS), F32),
-        ],
-        in_specs=[in_place] * 8,
-        out_specs=[on_chip] * 4,
+        out_shape=outs,
+        in_specs=[in_hbm] * 10,
+        out_specs=[on_chip] * 7,
         scratch_shapes=[
-            vmem((vocab, D), F32), vmem((vocab, D), F32), vmem((RANK, vocab), F32),
-            vmem((COLS, D), F32), vmem((COLS, D), F32), vmem((4, ROWS), F32),
+            vmem((vocab, D), F32), vmem((vocab, D), F32), vmem((vocab, D), F32),
+            vmem((RANK, vocab), F32), vmem((COLS, D), F32), vmem((COLS, D), F32),
+            vmem((4, ROWS), F32), vmem((4, ROWS), F32),
             vmem((PLANE, PAIR, D), F32), vmem((PLANE, PAIR, D), F32),
             vmem((1, PAIR, D), F32), vmem((RING, PAIR, D), F32),
             vmem((1, PAIR, D), F32), vmem((PLANE, PAIR, D), F32),
+            vmem((RANK, D), F32),
             vmem((N, ROWS, 1, WIDE), F32),
             vmem((N, 2, ROWS, COLS), F32), vmem((N, 2, ROWS, COLS), F32),
             vmem((N, ROWS, COLS), F32), vmem((N, ROWS, COLS), F32),
             vmem((1, COLS, TALL), F32), vmem((N, COLS, TALL), F32),
+            vmem((COLS, D), F32),
             vmem((1, ROWS, WIDE), BF16), vmem((N, ROWS, WIDE), BF16),
             vmem((N, 4, ROWS), F32),
-            dma((9,)), dma((9,)), dma((2,)), dma((8,)),
+            dma((9,)), dma((9,)), dma((2,)), dma((10,)),
         ],
         compiler_params=pltpu.CompilerParams(
             collective_id=0, has_side_effects=True, vmem_limit_bytes=24 << 20
         ),
     )(
-        inner_embed, outer_embed, basis_t, inner_rows, outer_t, moment_t,
-        inner_norms, outer_norms,
-    )
-
-    outs = [
-        shape((vocab, D), F32), shape((vocab, D), F32), shape((COLS, D), F32),
-        shape((COLS, D), F32), shape((4, ROWS), F32), shape((4, ROWS), F32),
-    ]
+        *[
+            pltpu.with_memory_space_constraint(array, pltpu.HBM)
+            for array in (
+                inner_embed, outer_embed, moment_embed, basis_t, inner_rows, outer_t,
+                moment_t, inner_norms, outer_norms, moment_norms,
+            )
+        ]
+    )
+
     new_e, new_me, new_a, new_ma, new_n, new_mn, replica = pl.pallas_call(
-        finish,
-        out_shape=[*outs, shape((ROWS, 4 * D), BF16)],
-        in_specs=[on_chip] * 11,
+        write,
+        out_shape=outs,
+        in_specs=[on_chip] * 7,
         out_specs=[in_place] * 7,
-        scratch_shapes=[*[vmem(out.shape, F32) for out in outs], dma((7,))],
-        compiler_params=pltpu.CompilerParams(vmem_limit_bytes=16 << 20),
-    )(
-        coef, delta_t, rep, norm, outer_embed, moment_embed, basis_t, outer_t,
-        moment_t, outer_norms, moment_norms,
-    )
+        scratch_shapes=[dma((7,))],
+        compiler_params=pltpu.CompilerParams(vmem_limit_bytes=4 << 20),
+    )(*results)
     return new_e, new_me, new_a.T, new_ma.T, new_n, new_mn, replica
 
 

time: 56.9 us -> 47.1 us (0.83)
  local copies, waits for them, and re-layouts: 7.15 us -> 0 us
  Pallas kernels: 48.7 us -> 46.3 us
    unnamed x20 -> x0, local copies, waits for them, and re-layouts: 7.15 us -> none
    pallas_call x2, Pallas kernels: 48.7 us -> 46.3 us  [the longest x1 45 us: on_device(): pl.pallas_call(exchange, out_shape=outs, in_specs=[in_hbm] * 10, out_spec...]
where the time goes in v3:
time: 47.1 us; the launch traced here: 46.9 us
  Pallas kernels  46.3 us (98%)
  between operations  0.64 us (1%)
    pallas_call x1, Pallas kernels, on_device(): pl.pallas_call(exchange, out_shape=outs, in_specs=[in_hbm] * 10, out_spec...  45 us
    pallas_call x1, Pallas kernels, on_device(): pl.pallas_call(write, out_shape=outs, in_specs=[on_chip] * 7, out_specs=[...  1.3 us

profile of v3, /device:TPU:1, one launch (start us, length us, event | category | flops | bytes accessed | tf_op | source)
XLA Modules:
  0.0 46.9 jit_solution(12947766624316705356)
XLA Ops:
  0.6 45.0 %shard_map.153 = (f32[240,768]{1,0:T(8,128)S(1)}, f32[240,768]{1,0:T(8,128)S(1)}, f32[48,768]{1,0:T(8,128)S(1)}, f32[48,768]{1,0:T(8,128)S(1)}, f32[4,12]{1,0:T(...) custom-call(f32[1,240,768]{2,1,0:T(8,128)} %inner_e.1, f32[240,768]{1,0:T(8,128)} %outer_e.1, ...), custom_call_target="tpu_custom_call" | custom-call | tf_op jit(solution)/shard_map/pallas_call | solution.py:328
  45.6 1.3 %shard_map.154 = (f32[240,768]{1,0:T(8,128)}, f32[240,768]{1,0:T(8,128)}, f32[48,768]{1,0:T(8,128)}, f32[48,768]{1,0:T(8,128)}, f32[4,12]{1,0:T(4,128)}, /*index=5*/f32[4,12]{1,0:T(4,128)}, bf16[12,3072]{1,0:T(8,128)(2,1)}) custom-call(f32[240,768]{1,0:T(8,128)S(1)} %get-tuple-element.21.refs_0_, f32[240,768]{1,0:T(8,128)S(1)} %get-tuple-element.22.refs_1_, ...), custom_call_target="tpu_custom_call" | custom-call | tf_op jit(solution)/shard_map/pallas_call | solution.py:363

commit v4 on v3

--- a/solution.py
+++ b/solution.py
@@ -24,7 +24,7 @@
 F32 = jnp.float32
 BF16 = jnp.bfloat16
 
-C1, CZ, C3, P1, W, NR, SW, AG, RP = range(9)
+C1, CZ, C3, P1, W, NR, SW, S2, AG, RP = range(10)
 L_IE, L_OE, L_ME, L_BA, L_OA, L_MA, L_IA, L_IN, L_ON, L_MN = range(10)
 
 G_STEPS = (4, 5, 3, 6, 2, 7, 1)
@@ -42,19 +42,36 @@
     return (outer - (delta + 0.5 * moment_new), moment_new)
 
 
+def inside(g):
+    return jnp.logical_and(g >= 2, g <= 5)
+
+
+def turned(g, half, x):
+    low = jnp.where(half == 0, g, 7 - g)
+    turn = jnp.where(inside(g), g - 2, jnp.where(low < 2, low, low - 4))
+    high = lax.rem(x // 2 + turn // 2, 2)
+    return 2 * high + lax.rem(lax.rem(x, 2) + lax.rem(turn, 2), 2)
+
+
 def across(g, b):
     half, x = b // 4, lax.rem(b, 4)
-    inner = jnp.logical_and(g >= 2, g <= 5)
-    low = jnp.where(half == 0, g, 7 - g)
-    outer_turn = jnp.where(low < 2, low, low - 4)
-    turn = jnp.where(inner, g - 2, outer_turn)
-    high, bit = turn // 2, lax.rem(turn, 2)
-    x_high, x_bit = x // 2, lax.rem(x, 2)
-    moved = 2 * lax.rem(x_high + high, 2) + lax.rem(x_bit + bit, 2)
-    return (
-        jnp.where(inner, g, 7 - g),
-        4 * jnp.where(inner, half, 1 - half) + moved,
-    )
+    to_half = jnp.where(inside(g), half, 1 - half)
+    return jnp.where(inside(g), g, 7 - g), 4 * to_half + turned(g, half, x)
+
+
+def second(g):
+    return jnp.where(
+        inside(g), lax.rem(g + 4, N), jnp.where(g < 4, g + 2, g - 2)
+    )
+
+
+def second_from(g, b):
+    half, x = b // 4, lax.rem(b, 4)
+    owner = jnp.where(
+        inside(g), jnp.where(g < 4, g - 2, g + 2), lax.rem(g + 4, N)
+    )
+    from_half = jnp.where(inside(owner), half, 1 - half)
+    return owner, 4 * from_half + turned(owner, from_half, x)
 
 
 def exchange(
@@ -62,7 +79,7 @@
     o_e, o_me, o_a, o_ma, o_n, o_mn, rep,
     v_ie, v_oe, v_me, v_ba, v_oa, v_ma, v_on, v_mn,
     c_part, r_c1, c_own, r_cz, c_fin, r_c3, coef,
-    r_p1, w_out, r_w, d_out, r_d, d_all, r_ag, delta_t, rp_out, r_rp, r_norm,
+    r_p1, w_out, r_w, d_out, r_d, r_d2, d_all, r_ag, delta_t, rp_out, r_rp, r_norm,
     send, recv, once, local,
 ):
     g = lax.axis_index("group")
@@ -72,6 +89,7 @@
     x, y, core = p // 8, lax.rem(p // 2, 4), lax.rem(p, 2)
     z = N * half + g
     far_g, far_b = across(g, b)
+    from_g, from_b = second_from(g, b)
 
     def in_plane(step):
         i, j, k = step
@@ -85,6 +103,10 @@
     to_ring = [(lax.rem(q, N), PLANE * (q // N) + p) for q in ring]
     to_line = [(q, s) for q in line]
     to_swap = [(far_g, N * far_b + q) for q in turns]
+    to_second = [(second(g), N * far_b + q) for q in turns]
+    to_near = [
+        (4 * (g // 4) + lax.rem(g + k, 4), s) for k in (2, 1, 3)
+    ]
     crossing = jnp.logical_or(far_b != b, far_g != g)
 
     barrier = pltpu.get_barrier_semaphore()
@@ -92,7 +114,7 @@
     def greet(device):
         pl.semaphore_signal(barrier, inc=1, device_id=device, device_id_type=MESH)
 
-    for device in to_ring + to_plane + to_swap[1:]:
+    for device in to_ring + to_swap[1:] + to_plane:
         greet(device)
 
     @pl.when(crossing)
@@ -217,7 +239,12 @@
         total = total + (outer_wide - r_p1[j, :, 0, :])
     delta = total * (1.0 / N)
     for j in range(N):
-        d_out[j] = delta[:, COLS * j : COLS * (j + 1)]
+        chunk = delta[:, COLS * j : COLS * (j + 1)]
+        d_out[j] = jnp.concatenate(
+            [chunk[: ROWS // 2, :], chunk[ROWS // 2 :, :]], axis=1
+        )
+    for k in range(N):
+        put(d_out.at[turns[k]], r_d2.at[a], S2, to_second[k])
     swap(d_out, r_d, SW, 1)
     replica = nesterov(outer_wide, mom_wide, delta)[0].astype(BF16)
     rp_out[0] = replica
@@ -235,12 +262,18 @@
         total = total + (outer_norm - r_norm[j])
     o_n[...], o_mn[...] = nesterov(outer_norm, v_mn[...], total * (1.0 / N))
 
+    def gather(ref, turn, rows):
+        parts = []
+        for j in range(N):
+            parts += [ref[j, :, :COLS], ref[j, :, COLS:]]
+        tall = jnp.concatenate(parts, axis=0).T
+        d_all[turn] = tall
+        for device in to_near:
+            put(d_all.at[turn], r_ag.at[rows], AG, device)
+        r_ag[rows] = tall
+
     swap_arrived(r_d, SW)
-    tall = jnp.concatenate([r_d[j] for j in range(N)], axis=0).T
-    d_all[0] = tall
-    for device in to_line:
-        put(d_all.at[0], r_ag.at[far_b], AG, device)
-    r_ag[far_b] = tall
+    gather(r_d, 0, far_b)
 
     arrived(r_cz, CZ)
     row = r_cz[0]
@@ -251,6 +284,9 @@
     for device in to_plane:
         put(c_fin.at[0], r_c3.at[p], C3, device)
     r_c3[p] = row
+
+    whole(r_d2, S2, N).wait_recv()
+    gather(r_d2, 1, from_b)
 
     arrived(r_rp, RP)
     for j in range(N):
@@ -269,18 +305,17 @@
     ) * SCALE
     o_e[...], o_me[...] = nesterov(v_oe[...], v_me[...], change)
 
-    arrived(r_ag, AG)
+    whole(r_ag, AG, 6).wait_recv()
     for j in range(N):
         delta_t[:, TALL * j : TALL * (j + 1)] = r_ag[j]
     o_a[...], o_ma[...] = nesterov(v_oa[...], v_ma[...], delta_t[...])
 
     for ref, phase in (
-        (r_c1, C1), (r_cz, CZ), (r_c3, C3), (r_p1, P1), (r_norm, NR), (r_ag, AG),
-        (r_rp, RP),
+        (r_c1, C1), (r_cz, CZ), (r_c3, C3), (r_p1, P1), (r_norm, NR), (r_rp, RP),
     ):
         whole(ref, phase, ref.shape[0] - 1).wait_send()
-    for ref, phase in ((r_w, W), (r_d, SW)):
-        whole(ref, phase, N - 1).wait_send()
+    for ref, phase, count in ((r_w, W, N - 1), (r_d, SW, N - 1), (r_d2, S2, N), (r_ag, AG, 6)):
+        whole(ref, phase, count).wait_send()
 
     @pl.when(crossing)
     def _():
@@ -340,12 +375,13 @@
             vmem((RANK, D), F32),
             vmem((N, ROWS, 1, WIDE), F32),
             vmem((N, 2, ROWS, COLS), F32), vmem((N, 2, ROWS, COLS), F32),
-            vmem((N, ROWS, COLS), F32), vmem((N, ROWS, COLS), F32),
-            vmem((1, COLS, TALL), F32), vmem((N, COLS, TALL), F32),
+            vmem((N, ROWS // 2, 2 * COLS), F32), vmem((N, ROWS // 2, 2 * COLS), F32),
+            vmem((N, ROWS // 2, 2 * COLS), F32),
+            vmem((2, COLS, TALL), F32), vmem((N, COLS, TALL), F32),
             vmem((COLS, D), F32),
             vmem((1, ROWS, WIDE), BF16), vmem((N, ROWS, WIDE), BF16),
             vmem((N, 4, ROWS), F32),
-            dma((9,)), dma((9,)), dma((2,)), dma((10,)),
+            dma((10,)), dma((10,)), dma((2,)), dma((10,)),
         ],
         compiler_params=pltpu.CompilerParams(
             collective_id=0, has_side_effects=True, vmem_limit_bytes=24 << 20

time: 47.1 us -> 45 us (0.955)
  Pallas kernels: 46.3 us -> 44.2 us
    pallas_call x1, Pallas kernels: 45 us -> 42.9 us  [on_device(): pl.pallas_call(exchange, out_shape=outs, in_specs=[in_hbm] * 10, out_spec...]
where the time goes in v4:
time: 45 us; the launch traced here: 44.9 us
  Pallas kernels  44.2 us (98%)
  between operations  0.64 us (1%)
    pallas_call x1, Pallas kernels, on_device(): pl.pallas_call(exchange, out_shape=outs, in_specs=[in_hbm] * 10, out_spec...  42.9 us
    pallas_call x1, Pallas kernels, on_device(): pl.pallas_call(write, out_shape=outs, in_specs=[on_chip] * 7, out_specs=[...  1.3 us

profile of v4, /device:TPU:1, one launch (start us, length us, event | category | flops | bytes accessed | tf_op | source)
XLA Modules:
  0.0 44.9 jit_solution(13096289700799627962)
XLA Ops:
  0.6 42.9 %shard_map.153 = (f32[240,768]{1,0:T(8,128)S(1)}, f32[240,768]{1,0:T(8,128)S(1)}, f32[48,768]{1,0:T(8,128)S(1)}, f32[48,768]{1,0:T(8,128)S(1)}, f32[4,12]{1,0:T(...) custom-call(f32[1,240,768]{2,1,0:T(8,128)} %inner_e.1, f32[240,768]{1,0:T(8,128)} %outer_e.1, ...), custom_call_target="tpu_custom_call" | custom-call | tf_op jit(solution)/shard_map/pallas_call | solution.py:363
  43.6 1.3 %shard_map.154 = (f32[240,768]{1,0:T(8,128)}, f32[240,768]{1,0:T(8,128)}, f32[48,768]{1,0:T(8,128)}, f32[48,768]{1,0:T(8,128)}, f32[4,12]{1,0:T(4,128)}, /*index=5*/f32[4,12]{1,0:T(4,128)}, bf16[12,3072]{1,0:T(8,128)(2,1)}) custom-call(f32[240,768]{1,0:T(8,128)S(1)} %get-tuple-element.21.refs_0_, f32[240,768]{1,0:T(8,128)S(1)} %get-tuple-element.22.refs_1_, ...), custom_call_target="tpu_custom_call" | custom-call | tf_op jit(solution)/shard_map/pallas_call | solution.py:399

commit v5 on v4

--- a/solution.py
+++ b/solution.py
@@ -17,6 +17,7 @@
 COLS = 48
 WIDE = N * COLS
 TALL = N * ROWS
+LEFT = 36
 PAIR = RANK // PLANE
 MESH = pl.DeviceIdType.MESH
 HIGHEST = lax.Precision.HIGHEST
@@ -104,8 +105,9 @@
     to_line = [(q, s) for q in line]
     to_swap = [(far_g, N * far_b + q) for q in turns]
     to_second = [(second(g), N * far_b + q) for q in turns]
+    turn_first = jnp.where(lax.rem(g, 4) < 2, 3, 1)
     to_near = [
-        (4 * (g // 4) + lax.rem(g + k, 4), s) for k in (2, 1, 3)
+        (4 * (g // 4) + lax.rem(g + k, 4), s) for k in (turn_first, 2, 4 - turn_first)
     ]
     crossing = jnp.logical_or(far_b != b, far_g != g)
 
@@ -267,13 +269,15 @@
         for j in range(N):
             parts += [ref[j, :, :COLS], ref[j, :, COLS:]]
         tall = jnp.concatenate(parts, axis=0).T
+        rest = [tall[LEFT:, 32 * j : 32 * (j + 1)] for j in range(3)]
+        tall = jnp.concatenate(
+            [tall[:LEFT, :], jnp.concatenate(rest, axis=0)], axis=1
+        )
         d_all[turn] = tall
         for device in to_near:
             put(d_all.at[turn], r_ag.at[rows], AG, device)
         r_ag[rows] = tall
 
-    swap_arrived(r_d, SW)
-    gather(r_d, 0, far_b)
 
     arrived(r_cz, CZ)
     row = r_cz[0]
@@ -285,6 +289,8 @@
         put(c_fin.at[0], r_c3.at[p], C3, device)
     r_c3[p] = row
 
+    swap_arrived(r_d, SW)
+    gather(r_d, 0, far_b)
     whole(r_d2, S2, N).wait_recv()
     gather(r_d2, 1, from_b)
 
@@ -307,7 +313,10 @@
 
     whole(r_ag, AG, 6).wait_recv()
     for j in range(N):
-        delta_t[:, TALL * j : TALL * (j + 1)] = r_ag[j]
+        packed = r_ag[j]
+        rest = [packed[12 * i : 12 * (i + 1), TALL:] for i in range(3)]
+        delta_t[:LEFT, TALL * j : TALL * (j + 1)] = packed[:, :TALL]
+        delta_t[LEFT:, TALL * j : TALL * (j + 1)] = jnp.concatenate(rest, axis=1)
     o_a[...], o_ma[...] = nesterov(v_oa[...], v_ma[...], delta_t[...])
 
     for ref, phase in (
@@ -377,7 +386,7 @@
             vmem((N, 2, ROWS, COLS), F32), vmem((N, 2, ROWS, COLS), F32),
             vmem((N, ROWS // 2, 2 * COLS), F32), vmem((N, ROWS // 2, 2 * COLS), F32),
             vmem((N, ROWS // 2, 2 * COLS), F32),
-            vmem((2, COLS, TALL), F32), vmem((N, COLS, TALL), F32),
+            vmem((2, LEFT, 128), F32), vmem((N, LEFT, 128), F32),
             vmem((COLS, D), F32),
             vmem((1, ROWS, WIDE), BF16), vmem((N, ROWS, WIDE), BF16),
             vmem((N, 4, ROWS), F32),

time: 45 us -> 44.1 us (0.980)
  Pallas kernels: 44.2 us -> 43.3 us
    pallas_call x1, Pallas kernels: 42.9 us -> 42 us  [on_device(): pl.pallas_call(exchange, out_shape=outs, in_specs=[in_hbm] * 10, out_spec...]
where the time goes in v5:
time: 44.1 us; the launch traced here: 43.9 us
  Pallas kernels  43.3 us (98%)
  between operations  0.64 us (1%)
    pallas_call x1, Pallas kernels, on_device(): pl.pallas_call(exchange, out_shape=outs, in_specs=[in_hbm] * 10, out_spec...  42 us
    pallas_call x1, Pallas kernels, on_device(): pl.pallas_call(write, out_shape=outs, in_specs=[on_chip] * 7, out_specs=[...  1.3 us

profile of v5, /device:TPU:1, one launch (start us, length us, event | category | flops | bytes accessed | tf_op | source)
XLA Modules:
  0.0 43.9 jit_solution(4992887166886834952)
XLA Ops:
  0.6 42.0 %shard_map.153 = (f32[240,768]{1,0:T(8,128)S(1)}, f32[240,768]{1,0:T(8,128)S(1)}, f32[48,768]{1,0:T(8,128)S(1)}, f32[48,768]{1,0:T(8,128)S(1)}, f32[4,12]{1,0:T(...) custom-call(f32[1,240,768]{2,1,0:T(8,128)} %inner_e.1, f32[240,768]{1,0:T(8,128)} %outer_e.1, ...), custom_call_target="tpu_custom_call" | custom-call | tf_op jit(solution)/shard_map/pallas_call | solution.py:372
  42.6 1.3 %shard_map.154 = (f32[240,768]{1,0:T(8,128)}, f32[240,768]{1,0:T(8,128)}, f32[48,768]{1,0:T(8,128)}, f32[48,768]{1,0:T(8,128)}, f32[4,12]{1,0:T(4,128)}, /*index=5*/f32[4,12]{1,0:T(4,128)}, bf16[12,3072]{1,0:T(8,128)(2,1)}) custom-call(f32[240,768]{1,0:T(8,128)S(1)} %get-tuple-element.21.refs_0_, f32[240,768]{1,0:T(8,128)S(1)} %get-tuple-element.22.refs_1_, ...), custom_call_target="tpu_custom_call" | custom-call | tf_op jit(solution)/shard_map/pallas_call | solution.py:408

commit v6 on v5

--- a/solution.py
+++ b/solution.py
@@ -19,6 +19,7 @@
 TALL = N * ROWS
 LEFT = 36
 PAIR = RANK // PLANE
+PARTS = 3
 MESH = pl.DeviceIdType.MESH
 HIGHEST = lax.Precision.HIGHEST
 SCALE = 1.0 / math.sqrt(RANK * VOCAB)
@@ -341,8 +342,16 @@
 
 def write(*refs):
     sems = refs[-1]
+    pairs = []
+    for src, dst in zip(refs[:7], refs[7:14]):
+        rows = src.shape[0]
+        step = rows // PARTS if rows % (8 * PARTS) == 0 else rows
+        for first in range(0, rows, step):
+            part = pl.ds(first, step)
+            pairs.append((src.at[part, :], dst.at[part, :]))
     copies = [
-        pltpu.make_async_copy(refs[i], refs[7 + i], sems.at[i]) for i in range(7)
+        pltpu.make_async_copy(src, dst, sems.at[i])
+        for i, (src, dst) in enumerate(pairs)
     ]
     for copy in copies:
         copy.start()
@@ -410,7 +419,7 @@
         out_shape=outs,
         in_specs=[on_chip] * 7,
         out_specs=[in_place] * 7,
-        scratch_shapes=[dma((7,))],
+        scratch_shapes=[dma((7 * PARTS,))],
         compiler_params=pltpu.CompilerParams(vmem_limit_bytes=4 << 20),
     )(*results)
     return new_e, new_me, new_a.T, new_ma.T, new_n, new_mn, replica

time: 44.1 us -> 44.2 us (level)
  no operation moved by 1% of the time
where the time goes in v6:
time: 44.2 us; the launch traced here: 44.1 us
  Pallas kernels  43.4 us (98%)
  between operations  0.64 us (1%)
    pallas_call x1, Pallas kernels, on_device(): pl.pallas_call(exchange, out_shape=outs, in_specs=[in_hbm] * 10, out_spec...  42 us
    pallas_call x1, Pallas kernels, on_device(): pl.pallas_call(write, out_shape=outs, in_specs=[on_chip] * 7, out_specs=[...  1.42 us

profile of v6, /device:TPU:1, one launch (start us, length us, event | category | flops | bytes accessed | tf_op | source)
XLA Modules:
  0.0 44.1 jit_solution(8031697888732789928)
XLA Ops:
  0.6 42.0 %shard_map.153 = (f32[240,768]{1,0:T(8,128)S(1)}, f32[240,768]{1,0:T(8,128)S(1)}, f32[48,768]{1,0:T(8,128)S(1)}, f32[48,768]{1,0:T(8,128)S(1)}, f32[4,12]{1,0:T(...) custom-call(f32[1,240,768]{2,1,0:T(8,128)} %inner_e.1, f32[240,768]{1,0:T(8,128)} %outer_e.1, ...), custom_call_target="tpu_custom_call" | custom-call | tf_op jit(solution)/shard_map/pallas_call | solution.py:381
  42.6 1.4 %shard_map.154 = (f32[240,768]{1,0:T(8,128)}, f32[240,768]{1,0:T(8,128)}, f32[48,768]{1,0:T(8,128)}, f32[48,768]{1,0:T(8,128)}, f32[4,12]{1,0:T(4,128)}, /*index=5*/f32[4,12]{1,0:T(4,128)}, bf16[12,3072]{1,0:T(8,128)(2,1)}) custom-call(f32[240,768]{1,0:T(8,128)S(1)} %get-tuple-element.21.refs_0_, f32[240,768]{1,0:T(8,128)S(1)} %get-tuple-element.22.refs_1_, ...), custom_call_target="tpu_custom_call" | custom-call | tf_op jit(solution)/shard_map/pallas_call | solution.py:417
